TPU v7x, 32 devices: a whole 2x2x4 slice. The times are simulated.
32 devices in a mesh: row: 8 (over z, x), col: 4 (over y, core).
Axes of the slice: x: 2, y: 2, z: 4, core: 2. Of those that a mesh axis runs over, the one named last changes fastest.
Arguments:
- receptance: bfloat16 [2, 16384, 16384], P(None, 'row', 'col'), may hold values from -4 to 60, as said below
- coupling: int32 [2, 768], replicated, may hold values from 0 to 16383, as said below
Outputs:
- coupled: bfloat16 [2, 16384, 16384], P(None, 'row', 'col')
Inputs may be any that keep to these rules, and one draw needn't show every extreme that they name: `coupling`: row 0 holds 768 distinct body DOFs, all in the first half of the 16384 DOFs; row 1 holds 768 distinct cavity DOFs, all in the second half. `receptance`: the driving-point entry of every body or cavity DOF named in coupling (same response and excitation DOF) has real part 52 or more; every other real or imaginary part lies within -4 to 4.
All inputs are finite; a program needn't handle non-finite values.
Results may differ from a plain program's by a relative error of at most 0.015.
Values may be sent and summed in bfloat16 or wider, within the bound.
A program may use at most 320 MiB of HBM per device.

v0:
```python
import jax
import jax.numpy as jnp
from jax import lax
from jax.sharding import PartitionSpec as P

SWEEPS = 6


def select_rows(matrix, body_dof, cav_dof, offset, extent):
    count = body_dof.shape[0]
    both_dof = jnp.concatenate([body_dof, cav_dof]) - offset
    inside = (both_dof >= 0) & (both_dof < extent)
    clipped = jnp.clip(both_dof, 0, extent - 1)
    picked = jnp.take(matrix, clipped, axis=1).astype(jnp.float32)
    picked = jnp.where(inside[None, :, None], picked, jnp.zeros((), jnp.float32))
    return picked[:, :count, :] - picked[:, count:, :]


def select_columns(matrix, body_dof, cav_dof, offset, extent):
    positions = offset + lax.broadcasted_iota(jnp.int32, (extent, 1), 0)
    table = (positions == body_dof[None, :]).astype(jnp.float32) - (
        positions == cav_dof[None, :]
    ).astype(jnp.float32)
    table = table.astype(matrix.dtype)
    return jnp.einsum(
        "prc,cn->prn",
        matrix,
        table,
        preferred_element_type=jnp.float32,
        precision=lax.Precision.HIGHEST,
    )


def complex_times(mat_real, mat_imag, vec_real, vec_imag):
    hi = lax.Precision.HIGHEST
    out_real = jnp.dot(mat_real, vec_real, precision=hi) - jnp.dot(mat_imag, vec_imag, precision=hi)
    out_imag = jnp.dot(mat_real, vec_imag, precision=hi) + jnp.dot(mat_imag, vec_real, precision=hi)
    return (out_real, out_imag)


def local(receptance, coupling):
    tile_rows = receptance.shape[1]
    tile_cols = receptance.shape[2]
    row_index = lax.axis_index("row")
    col_index = lax.axis_index("col")
    body_dof = coupling[0]
    cav_dof = coupling[1]
    row_terms = select_rows(receptance, body_dof, cav_dof, row_index * tile_rows, tile_rows)
    rhs_local = lax.psum_scatter(
        row_terms.astype(jnp.bfloat16), "row", scatter_dimension=2, tiled=True
    ).astype(jnp.float32)
    solve_cols = rhs_local.shape[2]
    column_terms = select_columns(receptance, body_dof, cav_dof, col_index * tile_cols, tile_cols)
    left_full = lax.psum(column_terms.astype(jnp.bfloat16), "col")
    first_col = col_index * tile_cols + row_index * solve_cols
    inter_terms = select_columns(rhs_local, body_dof, cav_dof, first_col, solve_cols)
    interface = lax.psum(inter_terms, ("row", "col"))
    z_real = interface[0]
    z_imag = interface[1]
    diag_real = jnp.diagonal(z_real)
    diag_imag = jnp.diagonal(z_imag)
    modulus = diag_real * diag_real + diag_imag * diag_imag
    d_real = (diag_real / modulus)[:, None]
    d_imag = (-diag_imag / modulus)[:, None]

    def scale(part_real, part_imag):
        return (d_real * part_real - d_imag * part_imag, d_real * part_imag + d_imag * part_real)

    v_real = rhs_local[0]
    v_imag = rhs_local[1]
    x_real, x_imag = scale(v_real, v_imag)
    for sweep_index in range(SWEEPS):
        p_real, p_imag = complex_times(z_real, z_imag, x_real, x_imag)
        e_real, e_imag = scale(v_real - p_real, v_imag - p_imag)
        x_real = x_real + e_real
        x_imag = x_imag + e_imag
    weights = jnp.stack([x_real, x_imag]).astype(jnp.bfloat16)
    u_real = left_full[0]
    u_imag = left_full[1]
    column_piece = lax.all_gather(weights, "row", axis=2, tiled=True)
    p_real = column_piece[0]
    p_imag = column_piece[1]
    c_real = jnp.dot(u_real, p_real, preferred_element_type=jnp.float32) - jnp.dot(
        u_imag, p_imag, preferred_element_type=jnp.float32
    )
    c_imag = jnp.dot(u_real, p_imag, preferred_element_type=jnp.float32) + jnp.dot(
        u_imag, p_real, preferred_element_type=jnp.float32
    )
    recv_piece = receptance.astype(jnp.float32)
    return (recv_piece - jnp.stack([c_real, c_imag])).astype(jnp.bfloat16)


def solution(mesh):
    in_specs = (P(None, "row", "col"), P())
    out_specs = P(None, "row", "col")
    return jax.shard_map(local, mesh=mesh, in_specs=in_specs, out_specs=out_specs, check_vma=False)
```

profile of v0, /device:TPU:0, one launch (start us, length us, event | category | flops | bytes accessed | tf_op | source)
XLA Modules:
  0.0 973.6 jit_solution(2592334917314808475)
XLA Ops:
  7.4 93.4 %gather_fusion = bf16[1536,2,4096]{2,0,1:T(8,128)(2,1)} fusion(bf16[2,2048,4096]{2,1,0:T(8,128)(2,1)} %param.2, s32[2048]{0:T(1024)S(1)} %pad_clamp_fusion), kind=kCustom, calls=%fused_computation | custom fusion | bytes 50337792 | tf_op jit(solution)/shard_map/jit(_take)/gather | solution.py:14
  100.8 27.7 %select_bitcast_fusion = f32[2,1536,4096]{2,1,0:T(8,128)} fusion(bf16[1536,2,4096]{2,0,1:T(8,128)(2,1)} %gather_fusion, pred[1536]{0:T(1024)(128)(4,1)S(1)} %get-tuple-element.24, pred[1536]{0:T(1024)(128)(4,1)S(1)} %get-tuple-element.23), kind=kLoop, calls=%fused_computation.5 | loop fusion | flops 37748736 | bytes 75500544 | tf_op jit(solution)/shard_map/jit(_where)/select_n | solution.py:15
  128.5 21.2 %fusion.1 = bf16[2,768,4096]{2,1,0:T(8,128)(2,1)} fusion(f32[2,1536,4096]{2,1,0:T(8,128)} %select_bitcast_fusion), kind=kLoop, calls=%fused_computation.9 | loop fusion | flops 12582912 | bytes 62914560 | tf_op jit(solution)/shard_map/convert_element_type | solution.py:50
  149.8 207.7 %reduce-scatter.2.cloned.1.call-done = bf16[2,768,512]{2,1,0:T(8,128)(2,1)} async-done(((bf16[2,768,4096]{2,1,0:T(8,128)(2,1)}), bf16[2,768,512]{2,1,0:T(8,128)(2,1)}) %reduce-scatter.2.cloned.1.call-update) | async-done | bytes 1572880 | tf_op jit(solution)/shard_map/reduce_scatter | solution.py:49
  357.5 7.8 fusion.24
  365.4 31.4 %convert_bitcast_fusion = bf16[2,2048,768]{1,2,0:T(8,128)(2,1)} fusion(bf16[2,2048,4096]{2,1,0:T(8,128)(2,1)} %param.2, s32[4096]{0:T(1024)S(1)} %iota_add_fusion, s32[768]{0:T(1024)S(1)} %get-tuple-element.6, s32[768]{0:T(1024)S(1)} %get-tuple-element.5), kind=kOutput, calls=%fused_computation.15 | convolution fusion | flops 25791823872 | bytes 39868416 | tf_op jit(solution)/shard_map/prc,cn->prn/dot_general | solution.py:25
  400.3 108.9 %all-reduce.5.cloned.1.call-done = f32[2,768,768]{2,1,0:T(8,128)} async-done(((f32[2,768,768]{2,1,0:T(8,128)}), f32[2,768,768]{2,1,0:T(8,128)}) %all-reduce.5.cloned.1.call-update) | async-done | bytes 4718608 | tf_op jit(solution)/shard_map/psum | solution.py:57
  513.4 12.4 %gather_fusion.1 = f32[768]{0:T(1024)S(1)} fusion(f32[768,768]{1,0:T(8,128)} %get-tuple-element.9, s32[768]{0:T(1024)S(1)} %or_reduce_fusion), kind=kCustom, calls=%fused_computation.1 | custom fusion | bytes 12288 | tf_op jit(solution)/shard_map/jit(diagonal)/cond/branch_0_fun/gather | solution.py:60
  525.8 6.5 gather_fusion.2
  532.3 6.9 fusion.12
  539.2 6.9 fusion.14
  550.3 5.1 fusion.21
  567.2 4.8 subtract_add_fusion.3
  583.7 4.5 subtract_add_fusion.2
  600.2 4.3 subtract_add_fusion.1
  612.3 4.4 bitcast_subtract_fusion.7
  616.7 4.3 subtract_add_fusion
  633.0 4.5 fusion.35
  638.8 175.8 %all-gather.2.cloned.1.call-done = bf16[2,768,4096]{2,1,0:T(8,128)(2,1)} async-done(((bf16[2,768,512]{2,1,0:T(8,128)(2,1)}), bf16[2,768,4096]{2,1,0:T(8,128)(2,1)}) %all-gather.2.cloned.1.call-update) | async-done | bytes 12582928 | tf_op jit(solution)/shard_map/all_gather | solution.py:80
  814.6 23.2 %fusion.9 = f32[2048,4096]{1,0:T(8,128)} fusion(bf16[2,768,4096]{2,1,0:T(8,128)(2,1)} %all-gather.2.cloned.1.call-done, bf16[2,2048,768]{1,2,0:T(8,128)(2,1)} %all-reduce.3.cloned.1.call-done), kind=kOutput, calls=%fused_computation.20 | convolution fusion | flops 12884901888 | bytes 42991616 | tf_op jit(solution)/shard_map/dot_general | solution.py:86
  837.8 20.2 %fusion.8 = f32[2048,4096]{1,0:T(8,128)} fusion(bf16[2,768,4096]{2,1,0:T(8,128)(2,1)} %all-gather.2.cloned.1.call-done, bf16[2,2048,768]{1,2,0:T(8,128)(2,1)S(1)} %copy-done.2), kind=kOutput, calls=%fused_computation.19 | convolution fusion | flops 12884901888 | bytes 42991616 | tf_op jit(solution)/shard_map/dot_general | solution.py:83
  858.1 33.0 %add_bitcast_fusion = f32[1,2048,4096]{2,1,0:T(8,128)} fusion(f32[2048,4096]{1,0:T(8,128)} %fusion.9, bf16[2,768,4096]{2,1,0:T(8,128)(2,1)} %all-gather.2.cloned.1.call-done, bf16[2,2048,768]{1,2,0:T(8,128)(2,1)} %all-reduce.3.cloned.1.call-done), kind=kOutput, calls=%fused_computation.6 | convolution fusion | flops 12893290496 | bytes 76546048 | tf_op jit(solution)/shard_map/dot_general | solution.py:86
  891.0 33.3 %subtract_bitcast_fusion = f32[1,2048,4096]{2,1,0:T(8,128)} fusion(f32[2048,4096]{1,0:T(8,128)} %fusion.8, bf16[2,768,4096]{2,1,0:T(8,128)(2,1)} %all-gather.2.cloned.1.call-done, bf16[2,2048,768]{1,2,0:T(8,128)(2,1)} %all-reduce.3.cloned.1.call-done), kind=kOutput, calls=%fused_computation.7 | convolution fusion | flops 12893290496 | bytes 76546048 | tf_op jit(solution)/shard_map/dot_general | solution.py:83
  924.3 42.3 %fusion = bf16[2,2048,4096]{2,1,0:T(8,128)(2,1)} fusion(f32[1,2048,4096]{2,1,0:T(8,128)} %add_bitcast_fusion, f32[1,2048,4096]{2,1,0:T(8,128)} %subtract_bitcast_fusion, bf16[2,2048,4096]{2,1,0:T(8,128)(2,1)} %param.2), kind=kLoop, calls=%fused_computation.4 | loop fusion | flops 67108864 | bytes 134217728 | tf_op jit(solution)/shard_map/convert_element_type | solution.py:90
  (46 shorter events, 69.2 us)
Async XLA Ops:
  6.5 351.0 %reduce-scatter.2.cloned.1.call-start = ((), (), s32[]{:S(2)}) async-start(), calls=%async_computation.2 | async-start | bytes 14155776 | tf_op jit(solution)/shard_map/reduce_scatter | solution.py:49
  149.7 359.5 %all-reduce.5.cloned.1.call-start = ((), (), s32[]{:S(2)}) async-start(), calls=%async_computation.3 | async-start | bytes 9437184 | tf_op jit(solution)/shard_map/psum | solution.py:57
  365.4 273.4 %all-reduce.3.cloned.1.call-start = ((), (), s32[]{:S(2)}) async-start(), calls=%async_computation.1 | async-start | bytes 12582912 | tf_op jit(solution)/shard_map/psum | solution.py:54
  396.8 1.4 copy-start.1
  396.8 417.8 %all-gather.2.cloned.1.call-start = ((), (), s32[]{:S(2)}) async-start(), calls=%async_computation.4 | async-start | bytes 14155776 | tf_op jit(solution)/shard_map/all_gather | solution.py:80
  525.7 20.3 %slice-start = ((s8[4718592]{0:T(1024)(128)(4,1)}), s8[524288]{0:T(1024)(128)(4,1)S(1)}, s32[]{:S(2)}) async-start(s8[4718592]{0:T(1024)(128)(4,1)} %bitcast.150), calls=%async_computation.5 | async-start | bytes 1048576
  532.3 13.8 %slice-start.1 = ((s8[4718592]{0:T(1024)(128)(4,1)}), s8[4194304]{0:T(1024)(128)(4,1)S(1)}, s32[]{:S(2)}) async-start(s8[4718592]{0:T(1024)(128)(4,1)} %bitcast.150), calls=%async_computation.6 | async-start | bytes 8388608
  539.2 6.9 copy-start
  814.6 23.2 %copy-start.2 = (bf16[2,2048,768]{1,2,0:T(8,128)(2,1)S(1)}, bf16[2,2048,768]{1,2,0:T(8,128)(2,1)}, u32[]{:S(2)}) copy-start(bf16[2,2048,768]{1,2,0:T(8,128)(2,1)} %all-reduce.3.cloned.1.call-done) | copy-start | bytes 18874372
Sparse Core Ops, SparseCore 0:
  149.8 207.6 reduce-scatter.1
  365.5 143.7 all-reduce.4
  511.8 118.4 all-reduce.2
  638.9 175.7 all-gather.1
where the time goes:
time: 984 us; the launch traced here: 974 us
  waiting for transfers between devices  493 us (50%)
  matrix products  254 us (26%)
  local copies, waits for them, and re-layouts  119 us (12%)
  other arithmetic  94.7 us (10%)
  between operations  13.9 us (1%)
    reduce_scatter x1, waiting for transfers between devices, local(): lax.psum_scatter(row_terms.astype(jnp.bfloat16), 'row', scatter_dimension...  208 us
    all_gather x1, waiting for transfers between devices, local(): column_piece = lax.all_gather(weights, 'row', axis=2, tiled=True)  176 us
    psum x1, waiting for transfers between devices, local(): interface = lax.psum(inter_terms, ('row', 'col'))  109 us
    gather x1, local copies, waits for them, and re-layouts, select_rows(): picked = jnp.take(matrix, clipped, axis=1).astype(jnp.float32)  93.4 us
    convert_element_type x1, other arithmetic, local(): return (recv_piece - jnp.stack([c_real, c_imag])).astype(jnp.bfloat16)  42.3 us
    dot_general x2, matrix products, select_columns(): jnp.einsum('prc,cn->prn', matrix, table, preferred_element_type=jnp.float...  39.2 us
    dot_general x1, matrix products, local(): jnp.dot(u_imag, p_imag, preferred_element_type=jnp.float32)  33.3 us
    dot_general x1, matrix products, local(): jnp.dot(u_imag, p_real, preferred_element_type=jnp.float32)  33 us
  transfers between devices with their start and end apart: 4, of which 3 were waited for; matrix products, arithmetic and copies ran while one was open for 17% of the time, Pallas kernels for 0%

commit v1 on v0

--- a/solution.py
+++ b/solution.py
@@ -77,7 +77,19 @@
     weights = jnp.stack([x_real, x_imag]).astype(jnp.bfloat16)
     u_real = left_full[0]
     u_imag = left_full[1]
-    column_piece = lax.all_gather(weights, "row", axis=2, tiled=True)
+    then = jax.lax.axis_size("row")
+    latest = jax.lax.axis_index("row")
+    inter, h_now = (then, latest)
+    column_piece, work_now = (weights, 1)
+    while work_now < inter:
+        trail = []
+        for rr in range(inter):
+            trail.append((rr, rr ^ work_now))
+        z_new = jax.lax.ppermute(column_piece, "row", trail)
+        big = jnp.concatenate([column_piece, z_new], axis=2)
+        piece_out = jnp.concatenate([z_new, column_piece], 2)
+        column_piece = jnp.where(h_now & work_now == 0, big, piece_out)
+        work_now = 2 * work_now
     p_real = column_piece[0]
     p_imag = column_piece[1]
     c_real = jnp.dot(u_real, p_real, preferred_element_type=jnp.float32) - jnp.dot(

time: 984 us -> 1240 us (1.26)
  waiting for transfers between devices: 493 us -> 686 us
  local copies, waits for them, and re-layouts: 119 us -> 152 us
  other arithmetic: 94.7 us -> 118 us
    ppermute x0 -> x3, waiting for transfers between devices: none -> 338 us  [local(): z_new = jax.lax.ppermute(column_piece, 'row', trail)]
    all_gather x1 -> x0, waiting for transfers between devices: 176 us -> none  [local(): column_piece = lax.all_gather(weights, 'row', axis=2, tiled=True)]
    gather x1 -> x2, local copies, waits for them, and re-layouts: 93.4 us -> 126 us  [select_rows(): picked = jnp.take(matrix, clipped, axis=1).astype(jnp.float32)]
    psum x1, waiting for transfers between devices: 109 us -> 141 us  [local(): interface = lax.psum(inter_terms, ('row', 'col'))]
    select_n x0 -> x3, other arithmetic: none -> 24.6 us  [local(): column_piece = jnp.where(h_now & work_now == 0, big, piece_out)]
  transfers between devices with their start and end apart: 4 -> 6, of which waited for: 3 -> 5; matrix products, arithmetic and copies ran while one was open for 17% -> 4% of each run, Pallas kernels for 0% -> 0%
where the time goes in v1:
time: 1240 us; the launch traced here: 1230 us
  waiting for transfers between devices  686 us (55%)
  matrix products  255 us (21%)
  local copies, waits for them, and re-layouts  152 us (12%)
  other arithmetic  118 us (10%)
  between operations  15.6 us (1%)
    ppermute x3, waiting for transfers between devices, local(): z_new = jax.lax.ppermute(column_piece, 'row', trail)  338 us
    reduce_scatter x1, waiting for transfers between devices, local(): lax.psum_scatter(row_terms.astype(jnp.bfloat16), 'row', scatter_dimension...  207 us
    psum x1, waiting for transfers between devices, local(): interface = lax.psum(inter_terms, ('row', 'col'))  141 us
    gather x2, local copies, waits for them, and re-layouts, select_rows(): picked = jnp.take(matrix, clipped, axis=1).astype(jnp.float32)  126 us
    convert_element_type x1, other arithmetic, local(): return (recv_piece - jnp.stack([c_real, c_imag])).astype(jnp.bfloat16)  42.3 us
    dot_general x2, matrix products, select_columns(): jnp.einsum('prc,cn->prn', matrix, table, preferred_element_type=jnp.float...  39.3 us
    dot_general x1, matrix products, local(): jnp.dot(u_imag, p_imag, preferred_element_type=jnp.float32)  33.2 us
    dot_general x1, matrix products, local(): jnp.dot(u_imag, p_real, preferred_element_type=jnp.float32)  32.9 us
  transfers between devices with their start and end apart: 6, of which 5 were waited for; matrix products, arithmetic and copies ran while one was open for 4% of the time, Pallas kernels for 0%

profile of v1, /device:TPU:0, one launch (start us, length us, event | category | flops | bytes accessed | tf_op | source)
XLA Modules:
  0.0 1229.7 jit_solution(14727885001637479565)
XLA Ops:
  8.2 93.2 %gather_fusion = bf16[1536,2,4096]{2,0,1:T(8,128)(2,1)} fusion(bf16[2,2048,4096]{2,1,0:T(8,128)(2,1)} %param.2, s32[2048]{0:T(1024)S(1)} %pad_clamp_fusion), kind=kCustom, calls=%fused_computation | custom fusion | bytes 50337792 | tf_op jit(solution)/shard_map/jit(_take)/gather | solution.py:14
  101.5 32.8 %copy.4 = bf16[1536,2,4096]{0,2,1:T(8,128)(2,1)} copy(bf16[1536,2,4096]{2,0,1:T(8,128)(2,1)} %gather_fusion) | data formatting | bytes 50331648 | tf_op jit(solution)/shard_map/jit(_take)/gather | solution.py:14
  134.2 27.2 %select_bitcast_fusion = f32[2,1536,4096]{1,2,0:T(8,128)} fusion(bf16[1536,2,4096]{0,2,1:T(8,128)(2,1)} %copy.4, pred[1536]{0:T(1024)(128)(4,1)S(1)} %get-tuple-element.24, pred[1536]{0:T(1024)(128)(4,1)S(1)} %get-tuple-element.23), kind=kLoop, calls=%fused_computation.5 | loop fusion | flops 37748736 | bytes 75500544 | tf_op jit(solution)/shard_map/jit(_where)/select_n | solution.py:15
  161.5 21.5 %fusion.1 = bf16[2,768,4096]{1,2,0:T(8,128)(2,1)} fusion(f32[2,1536,4096]{1,2,0:T(8,128)} %select_bitcast_fusion), kind=kLoop, calls=%fused_computation.9 | loop fusion | flops 12582912 | bytes 62914560 | tf_op jit(solution)/shard_map/convert_element_type | solution.py:50
  183.0 207.1 %reduce-scatter.2.cloned.1.call-done = bf16[2,768,512]{1,2,0:T(8,128)(2,1)} async-done(((bf16[2,768,4096]{1,2,0:T(8,128)(2,1)}), bf16[2,768,512]{1,2,0:T(8,128)(2,1)}) %reduce-scatter.2.cloned.1.call-update) | async-done | bytes 1572880 | tf_op jit(solution)/shard_map/reduce_scatter | solution.py:49
  390.1 7.8 fusion.24
  401.3 140.8 %all-reduce.5.cloned.1.call-done = f32[2,768,768]{2,1,0:T(8,128)} async-done(((f32[2,768,768]{2,1,0:T(8,128)}), f32[2,768,768]{2,1,0:T(8,128)}) %all-reduce.5.cloned.1.call-update) | async-done | bytes 4718608 | tf_op jit(solution)/shard_map/psum | solution.py:57
  546.2 12.4 %gather_fusion.1 = f32[768]{0:T(1024)S(1)} fusion(f32[768,768]{1,0:T(8,128)} %get-tuple-element.9, s32[768]{0:T(1024)S(1)} %or_reduce_fusion), kind=kCustom, calls=%fused_computation.1 | custom fusion | bytes 12288 | tf_op jit(solution)/shard_map/jit(diagonal)/cond/branch_0_fun/gather | solution.py:60
  558.6 6.5 gather_fusion.2
  565.2 6.8 fusion.12
  571.9 6.8 fusion.14
  578.8 4.6 bitcast_subtract_fusion.11
  583.4 4.5 fusion.21
  672.8 33.5 %collective-permute-done = bf16[2,768,512]{1,2,0:T(8,128)(2,1)} collective-permute-done((bf16[2,768,512]{1,2,0:T(8,128)(2,1)S(1)}, bf16[2,768,512]{1,2,0:T(8,128)(2,1)}, u32[]{:S(2)}, u32[]{:S(2)}) %collective-permute-start) | collective-permute-done | bytes 1572896 | tf_op jit(solution)/shard_map/ppermute | solution.py:88
  710.5 66.7 %collective-permute-done.1 = bf16[2,768,1024]{1,2,0:T(8,128)(2,1)} collective-permute-done((bf16[2,768,1024]{1,2,0:T(8,128)(2,1)S(1)}, bf16[2,768,1024]{1,2,0:T(8,128)(2,1)}, u32[]{:S(2)}, u32[]{:S(2)}) %collective-permute-start.1) | collective-permute-done | bytes 3145760 | tf_op jit(solution)/shard_map/ppermute | solution.py:88
  777.1 7.3 maximum_select_fusion.1
  785.3 31.4 %convert_bitcast_fusion = bf16[2,2048,768]{1,2,0:T(8,128)(2,1)} fusion(bf16[2,2048,4096]{2,1,0:T(8,128)(2,1)} %param.2, s32[4096]{0:T(1024)S(1)} %iota_add_fusion, s32[768]{0:T(1024)S(1)} %get-tuple-element.6, s32[768]{0:T(1024)S(1)} %get-tuple-element.5), kind=kOutput, calls=%fused_computation.17 | convolution fusion | flops 25791823872 | bytes 39868416 | tf_op jit(solution)/shard_map/prc,cn->prn/dot_general | solution.py:25
  816.8 237.6 %collective-permute-done.2 = bf16[2,768,2048]{1,2,0:T(8,128)(2,1)} collective-permute-done((bf16[2,768,2048]{1,2,0:T(8,128)(2,1)}, bf16[2,768,2048]{1,2,0:T(8,128)(2,1)}, u32[]{:S(2)}, u32[]{:S(2)}) %collective-permute-start.2) | collective-permute-done | bytes 6291488 | tf_op jit(solution)/shard_map/ppermute | solution.py:88
  1054.4 14.1 %maximum_select_fusion = bf16[2,768,4096]{1,2,0:T(8,128)(2,1)} fusion(bf16[2,768,2048]{1,2,0:T(8,128)(2,1)} %collective-permute-done.2, bf16[2,768,2048]{1,2,0:T(8,128)(2,1)} %maximum_select_fusion.1, pred[]{:T(512)S(6)} %eq.68), kind=kLoop, calls=%fused_computation.10 | loop fusion | flops 56623104 | bytes 25165824 | tf_op jit(solution)/shard_map/jit(_where)/select_n | solution.py:91
  1068.5 22.6 %fusion.9 = f32[2048,4096]{1,0:T(8,128)} fusion(bf16[2,768,4096]{1,2,0:T(8,128)(2,1)} %maximum_select_fusion, bf16[2,2048,768]{1,2,0:T(8,128)(2,1)} %all-reduce.3.cloned.1.call-done), kind=kOutput, calls=%fused_computation.22 | convolution fusion | flops 12884901888 | bytes 42991616 | tf_op jit(solution)/shard_map/dot_general | solution.py:98
  1091.1 22.3 %fusion.8 = f32[2048,4096]{1,0:T(8,128)} fusion(bf16[2,768,4096]{1,2,0:T(8,128)(2,1)} %maximum_select_fusion, bf16[2,2048,768]{1,2,0:T(8,128)(2,1)} %all-reduce.3.cloned.1.call-done), kind=kOutput, calls=%fused_computation.21 | convolution fusion | flops 12884901888 | bytes 42991616 | tf_op jit(solution)/shard_map/dot_general | solution.py:95
  1113.4 32.9 %add_bitcast_fusion = f32[1,2048,4096]{2,1,0:T(8,128)} fusion(f32[2048,4096]{1,0:T(8,128)} %fusion.9, bf16[2,768,4096]{1,2,0:T(8,128)(2,1)} %maximum_select_fusion, bf16[2,2048,768]{1,2,0:T(8,128)(2,1)} %all-reduce.3.cloned.1.call-done), kind=kOutput, calls=%fused_computation.6 | convolution fusion | flops 12893290496 | bytes 76546048 | tf_op jit(solution)/shard_map/dot_general | solution.py:98
  1146.3 33.2 %subtract_bitcast_fusion = f32[1,2048,4096]{2,1,0:T(8,128)} fusion(f32[2048,4096]{1,0:T(8,128)} %fusion.8, bf16[2,768,4096]{1,2,0:T(8,128)(2,1)} %maximum_select_fusion, bf16[2,2048,768]{1,2,0:T(8,128)(2,1)} %all-reduce.3.cloned.1.call-done), kind=kOutput, calls=%fused_computation.7 | convolution fusion | flops 12893290496 | bytes 76546048 | tf_op jit(solution)/shard_map/dot_general | solution.py:95
  1179.5 42.3 %fusion = bf16[2,2048,4096]{2,1,0:T(8,128)(2,1)} fusion(f32[1,2048,4096]{2,1,0:T(8,128)} %add_bitcast_fusion, f32[1,2048,4096]{2,1,0:T(8,128)} %subtract_bitcast_fusion, bf16[2,2048,4096]{2,1,0:T(8,128)(2,1)} %param.2), kind=kLoop, calls=%fused_computation.4 | loop fusion | flops 67108864 | bytes 134217728 | tf_op jit(solution)/shard_map/convert_element_type | solution.py:102
  (55 shorter events, 98.0 us)
Async XLA Ops:
  7.4 382.8 %reduce-scatter.2.cloned.1.call-start = ((), (), s32[]{:S(2)}) async-start(), calls=%async_computation.2 | async-start | bytes 14155776 | tf_op jit(solution)/shard_map/reduce_scatter | solution.py:49
  183.0 359.1 %all-reduce.5.cloned.1.call-start = ((), (), s32[]{:S(2)}) async-start(), calls=%async_computation.3 | async-start | bytes 9437184 | tf_op jit(solution)/shard_map/psum | solution.py:57
  398.0 1.4 copy-start.3
  398.0 670.5 %all-reduce.3.cloned.1.call-start = ((), (), s32[]{:S(2)}) async-start(), calls=%async_computation.1 | async-start | bytes 12582912 | tf_op jit(solution)/shard_map/psum | solution.py:54
  558.6 20.2 %slice-start = ((s8[4718592]{0:T(1024)(128)(4,1)}), s8[524288]{0:T(1024)(128)(4,1)S(1)}, s32[]{:S(2)}) async-start(s8[4718592]{0:T(1024)(128)(4,1)} %bitcast.150), calls=%async_computation.4 | async-start | bytes 1048576
  565.2 13.6 %slice-start.1 = ((s8[4718592]{0:T(1024)(128)(4,1)}), s8[4194304]{0:T(1024)(128)(4,1)S(1)}, s32[]{:S(2)}) async-start(s8[4718592]{0:T(1024)(128)(4,1)} %bitcast.150), calls=%async_computation.5 | async-start | bytes 8388608
  571.9 6.9 copy-start
  670.4 0.9 copy-start.1
  670.4 1.1 copy-start.2
  671.6 34.8 %collective-permute-start = (bf16[2,768,512]{1,2,0:T(8,128)(2,1)S(1)}, bf16[2,768,512]{1,2,0:T(8,128)(2,1)}, u32[]{:S(2)}, u32[]{:S(2)}) collective-permute-start(bf16[2,768,512]{1,2,0:T(8,128)(2,1)S(1)} %pad_maximum_fusion), channel_id=1, source_target_pairs={{0,4},{4,0},{8,12},{12,8},{16,20},{20,16},{24,28},{28,24},{1,5},{5... | collective-permute-start | bytes 4718600 | tf_op jit(solution)/shard_map/ppermute | solution.py:88
  709.5 67.6 %collective-permute-start.1 = (bf16[2,768,1024]{1,2,0:T(8,128)(2,1)S(1)}, bf16[2,768,1024]{1,2,0:T(8,128)(2,1)}, u32[]{:S(2)}, u32[]{:S(2)}) collective-permute-start(bf16[2,768,1024]{1,2,0:T(8,128)(2,1)S(1)} %maximum_select_fusion.2), channel_id=1, source_target_pairs={{0,8},{4,12},{8,0},{12,4},{16,24},{20,28},{24,16},{28,20},{1,9},{5... | collective-permute-start | bytes 9437192 | tf_op jit(solution)/shard_map/ppermute | solution.py:88
  784.4 270.0 %collective-permute-start.2 = (bf16[2,768,2048]{1,2,0:T(8,128)(2,1)}, bf16[2,768,2048]{1,2,0:T(8,128)(2,1)}, u32[]{:S(2)}, u32[]{:S(2)}) collective-permute-start(bf16[2,768,2048]{1,2,0:T(8,128)(2,1)} %maximum_select_fusion.1), channel_id=1, source_target_pairs={{0,16},{4,20},{8,24},{12,28},{16,0},{20,4},{24,8},{28,12},{1,17},{... | collective-permute-start | bytes 18874376 | tf_op jit(solution)/shard_map/ppermute | solution.py:88
Sparse Core Ops, SparseCore 0:
  183.1 207.0 reduce-scatter.1
  398.1 143.9 all-reduce.4
Sparse Core Ops, SparseCore 1:
  816.8 118.5 all-reduce.2
